TPU v7x, 32 devices: a whole 2x2x4 slice. The times are simulated.
32 devices in a mesh: dp: 2 (over x), ctx: 16 (over z, y, core).
Axes of the slice: x: 2, y: 2, z: 4, core: 2. Of those that a mesh axis runs over, the one named last changes fastest.
Arguments:
- queries: bfloat16 [32, 4096, 128], P(None, ('dp', 'ctx')), parts along dimension 1, may hold values from -150 to 150
- query_pos: bfloat16 [32, 4096, 64], P(None, ('dp', 'ctx')), parts along dimension 1, may hold values from -300 to 300
- key_values: bfloat16 [4, 2, 4096, 128], P(None, None, ('dp', 'ctx')), parts along dimension 2, may hold values from -20 to 20
- latent: bfloat16 [4096, 512], P(('dp', 'ctx')), parts along dimension 0, may hold values from -6 to 6
- key_pos: bfloat16 [4096, 64], P(('dp', 'ctx')), parts along dimension 0, may hold values from -4 to 4
- key_upward_matrix: bfloat16 [32, 128, 512], P(None, None, 'ctx'), may hold values from -0.5 to 0.5
- value_upward_matrix: bfloat16 [32, 512, 128], P(None, 'ctx'), may hold values from -1 to 1
- segment_ids: int32 [4096], P(('dp', 'ctx')), parts along dimension 0, may hold values from 0 to 15, never falling along the last dimension, each value on 1 to 256 neighbouring positions
Outputs:
- student_out: bfloat16 [32, 4096, 128], P(None, ('dp', 'ctx')), parts along dimension 1
- token_error: float32 [4096], P(('dp', 'ctx')), parts along dimension 0
There are 2 independent parts, one for each index of `dp`. A program takes and returns all parts, laid end to end along the dimension named above; an argument that names none is the same for every part. Nothing has to cross between parts.
Inputs may be any that keep to these rules, and one draw needn't show every extreme that they name: `segment_ids`: each document covers at most 256 consecutive positions; ids never fall along the sequence.
All inputs are finite; a program needn't handle non-finite values.
Results may differ from a plain program's by a relative error of at most 0.0071.
Values may be sent and summed in bfloat16 or wider, within the bound.
A program may use at most 64 MiB of HBM per device.

v0:
```python
import math

import jax
import jax.numpy as jnp
from jax import lax
from jax.sharding import PartitionSpec as P

REACH = 2


def from_behind(block, axis, distance):
    devices = range(lax.axis_size(axis))
    route = [(i - distance, i) for i in devices if i - distance in devices]
    return lax.ppermute(block, axis, route)


def masked_softmax(scores, allowed):
    scores = jnp.where(allowed, scores, -jnp.inf)
    highest = jnp.max(scores, axis=-1, keepdims=True)
    raised = jnp.exp(scores - highest)
    return raised / jnp.sum(raised, axis=-1, keepdims=True)


def earlier_blocks(bundle):
    fetched = []
    current = bundle
    for distance in range(REACH):
        current = from_behind((current[0], current[1], current[2], current[3]), "ctx", 1)
        fetched.append(current)
    return fetched[::-1]


def shards(
    queries,
    query_pos,
    key_values,
    latent,
    key_pos,
    key_upward_matrix,
    value_upward_matrix,
    segment_ids,
):
    head_count, block_len, head_dim = queries.shape
    kv_count = key_values.shape[0]
    groups = head_count // kv_count
    device_index = lax.axis_index("ctx")
    own_index = device_index * block_len + jnp.arange(block_len, dtype=jnp.int32)
    bundle = (latent, key_pos, segment_ids, key_values)
    earlier = earlier_blocks(bundle)
    keys_latent = jnp.concatenate([blk[0] for blk in earlier] + [latent], 0)
    keys_pos = jnp.concatenate([blk[1] for blk in earlier] + [key_pos], 0)
    keys_seg = jnp.concatenate([blk[2] for blk in earlier] + [segment_ids], 0)
    key_index = (device_index - REACH) * block_len + jnp.arange(
        (REACH + 1) * block_len, dtype=jnp.int32
    )
    allowed = (
        (keys_seg[None, :] == segment_ids[:, None])
        & (key_index[None, :] <= own_index[:, None])
        & (key_index[None, :] >= 0)
    )
    query_latent = jnp.einsum(
        "htd,hdc->htc",
        queries,
        lax.all_gather(key_upward_matrix, "ctx", axis=2, tiled=True),
        preferred_element_type=jnp.float32,
    ).astype(jnp.bfloat16)
    student_scale = 1.0 / math.sqrt(head_dim + key_pos.shape[1])
    scores = jnp.einsum(
        "htc,lc->htl", query_latent, keys_latent, preferred_element_type=jnp.float32
    )
    scores = (
        scores + jnp.einsum("htp,lp->htl", query_pos, keys_pos, preferred_element_type=jnp.float32)
    ) * student_scale
    attention_weight_grid = masked_softmax(scores, allowed[None]).astype(jnp.bfloat16)
    latent_out = jnp.einsum(
        "htl,lc->htc", attention_weight_grid, keys_latent, preferred_element_type=jnp.float32
    ).astype(jnp.bfloat16)
    student_out = jnp.einsum(
        "htc,hcd->htd",
        latent_out,
        lax.all_gather(value_upward_matrix, "ctx", axis=1, tiled=True),
        preferred_element_type=jnp.float32,
    ).astype(jnp.bfloat16)
    pair_keys = jnp.concatenate([blk[3] for blk in earlier] + [key_values], 2)
    grouped = queries.reshape(kv_count, groups, block_len, head_dim)
    teacher_scores = jnp.einsum(
        "kgtd,kld->kgtl", grouped, pair_keys[:, 0], preferred_element_type=jnp.float32
    )
    teacher_scores = teacher_scores * (1.0 / math.sqrt(head_dim))
    teacher_weights = masked_softmax(teacher_scores, allowed[None, None]).astype(jnp.bfloat16)
    teacher_out = jnp.einsum(
        "kgtl,kld->kgtd", teacher_weights, pair_keys[:, 1], preferred_element_type=jnp.float32
    )
    teacher_out = teacher_out.astype(jnp.bfloat16).reshape(head_count, block_len, head_dim)
    difference = student_out.astype(jnp.float32) - teacher_out.astype(jnp.float32)
    token_error = jnp.mean(difference * difference, axis=(0, 2))
    return (student_out, token_error)


def solution(mesh):
    placed = (
        P(None, ("dp", "ctx"), None),
        P(None, ("dp", "ctx"), None),
        P(None, None, ("dp", "ctx"), None),
        P(("dp", "ctx"), None),
        P(("dp", "ctx"), None),
        P(None, None, "ctx"),
        P(None, "ctx", None),
        P(("dp", "ctx")),
    )
    return jax.shard_map(
        shards,
        mesh=mesh,
        in_specs=placed,
        out_specs=(P(None, ("dp", "ctx"), None), P(("dp", "ctx"))),
        check_vma=False,
    )
```

profile of v0, /device:TPU:0, one launch (start us, length us, event | category | flops | bytes accessed | tf_op | source)
XLA Modules:
  0.0 143.6 jit_solution(4727479281196717908)
XLA Ops:
  7.2 0.0 copy-start
  7.2 0.0 copy-start.1
  7.2 0.0 all-gather.3.cloned.1.call-start
  7.2 0.7 all-gather.3.cloned.1.call-update
  7.9 0.0 all-gather.5.cloned.1.call-start
  8.0 0.7 all-gather.5.cloned.1.call-update
  8.7 2.4 %collective-permute-start = (s32[128]{0:T(128)}, s32[128]{0:T(128)S(1)}, u32[]{:S(2)}, u32[]{:S(2)}) collective-permute-start(s32[128]{0:T(128)} %param.15), channel_id=1, source_target_pairs={{0,1},{1,2},{2,3},{3,4},{4,5},{5,6},{6,7},{7,8},{8,9},{9,10},{10,1... | collective-permute-start | bytes 1544 | tf_op jit(solution)/shard_map/ppermute | solution.py:14
  11.1 1.0 copy.12
  12.1 4.5 %collective-permute-start.6 = (bf16[4,2,128,128]{3,2,0,1:T(8,128)(2,1)S(1)}, bf16[4,2,128,128]{3,2,0,1:T(8,128)(2,1)S(1)}, u32[]{:S(2)}, u32[]{:S(2)}) collective-permute-start(bf16[4,2,128,128]{3,2,0,1:T(8,128)(2,1)S(1)} %copy.12), channel_id=1, source_target_pairs={{0,1},{1,2},{2,3},{3,4},{4,5},{5,6},{6,7},{7,8},{8,9},{9,10},{10,1... | collective-permute-start | bytes 786440 | tf_op jit(solution)/shard_map/ppermute | solution.py:14
  16.6 1.9 %collective-permute-start.2 = (bf16[128,512]{1,0:T(8,128)(2,1)}, bf16[128,512]{1,0:T(8,128)(2,1)S(1)}, u32[]{:S(2)}, u32[]{:S(2)}) collective-permute-start(bf16[128,512]{1,0:T(8,128)(2,1)} %param.11), channel_id=1, source_target_pairs={{0,1},{1,2},{2,3},{3,4},{4,5},{5,6},{6,7},{7,8},{8,9},{9,10},{10,1... | collective-permute-start | bytes 393224 | tf_op jit(solution)/shard_map/ppermute | solution.py:14
  18.5 3.5 %collective-permute-start.4 = (bf16[128,64]{0,1:T(8,128)(2,1)}, bf16[128,64]{0,1:T(8,128)(2,1)S(1)}, u32[]{:S(2)}, u32[]{:S(2)}) collective-permute-start(bf16[128,64]{0,1:T(8,128)(2,1)} %param.12), channel_id=1, source_target_pairs={{0,1},{1,2},{2,3},{3,4},{4,5},{5,6},{6,7},{7,8},{8,9},{9,10},{10,1... | collective-permute-start | bytes 49160 | tf_op jit(solution)/shard_map/ppermute | solution.py:14
  22.1 0.0 collective-permute-done
  22.1 1.9 %collective-permute-start.1 = (s32[128]{0:T(128)S(1)}, s32[128]{0:T(128)S(1)}, u32[]{:S(2)}, u32[]{:S(2)}) collective-permute-start(s32[128]{0:T(128)S(1)} %collective-permute-done), channel_id=1, source_target_pairs={{0,1},{1,2},{2,3},{3,4},{4,5},{5,6},{6,7},{7,8},{8,9},{9,10},{10,1... | collective-permute-start | bytes 1544 | tf_op jit(solution)/shard_map/ppermute | solution.py:14
  24.0 0.8 collective-permute-done.1
  24.8 0.7 pad_add_fusion
  25.5 0.0 collective-permute-done.4
  25.5 3.4 %collective-permute-start.5 = (bf16[128,64]{0,1:T(8,128)(2,1)S(1)}, bf16[128,64]{0,1:T(8,128)(2,1)S(1)}, u32[]{:S(2)}, u32[]{:S(2)}) collective-permute-start(bf16[128,64]{0,1:T(8,128)(2,1)S(1)} %collective-permute-done.4), channel_id=1, source_target_pairs={{0,1},{1,2},{2,3},{3,4},{4,5},{5,6},{6,7},{7,8},{8,9},{9,10},{10,1... | collective-permute-start | bytes 49160 | tf_op jit(solution)/shard_map/ppermute | solution.py:14
  28.9 0.8 and_and_fusion
  29.7 0.2 copy.11
  29.9 0.0 collective-permute-done.6
  29.9 4.2 %collective-permute-start.7 = (bf16[4,2,128,128]{3,2,0,1:T(8,128)(2,1)S(1)}, bf16[4,2,128,128]{3,2,0,1:T(8,128)(2,1)S(1)}, u32[]{:S(2)}, u32[]{:S(2)}) collective-permute-start(bf16[4,2,128,128]{3,2,0,1:T(8,128)(2,1)S(1)} %collective-permute-done.6), channel_id=1, source_target_pairs={{0,1},{1,2},{2,3},{3,4},{4,5},{5,6},{6,7},{7,8},{8,9},{9,10},{10,1... | collective-permute-start | bytes 786440 | tf_op jit(solution)/shard_map/ppermute | solution.py:14
  34.1 0.0 collective-permute-done.5
  34.1 4.7 %fusion.28 = f32[384,32,128]{0,2,1:T(8,128)} fusion(bf16[32,128,64]{1,2,0:T(8,128)(2,1)} %param.9, bf16[128,64]{0,1:T(8,128)(2,1)} %param.12, bf16[128,64]{0,1:T(8,128)(2,1)S(1)} %collective-permute-done.4, bf16[128,64]{0,1:T(8,128)(2,1)S(1)} %collective-permute-done.5), kind=kOutput, calls=%fused_computation.34 | convolution fusion | flops 201474048 | bytes 6864896 | tf_op jit(solution)/shard_map/htp,lp->htl/dot_general | solution.py:72
  38.9 0.0 collective-permute-done.2
  38.9 1.9 %collective-permute-start.3 = (bf16[128,512]{1,0:T(8,128)(2,1)S(1)}, bf16[128,512]{1,0:T(8,128)(2,1)S(1)}, u32[]{:S(2)}, u32[]{:S(2)}) collective-permute-start(bf16[128,512]{1,0:T(8,128)(2,1)S(1)} %collective-permute-done.2), channel_id=1, source_target_pairs={{0,1},{1,2},{2,3},{3,4},{4,5},{5,6},{6,7},{7,8},{8,9},{9,10},{10,1... | collective-permute-start | bytes 393224 | tf_op jit(solution)/shard_map/ppermute | solution.py:14
  40.8 0.0 collective-permute-done.7
  40.9 0.0 copy-done.1
  40.9 0.0 copy-done
  40.9 4.6 %fusion.42 = (f32[4,8,128]{2,1,0:T(8,128)S(1)}, f32[4,8,128,384]{2,3,1,0:T(8,128)}) fusion(pred[128,384]{0,1:T(8,128)(4,1)S(1)} %copy.11, bf16[4,8,128,128]{3,2,1,0:T(8,128)(2,1)S(1)} %bitcast.61, bf16[4,2,384,128]{3,2,0,1:T(8,128)(2,1)S(1)} %constant_dynamic-update-slice_fusion), kind=kOutput, calls=%fused_computation.54 | convolution fusion | flops 408945024 | bytes 7798784 | tf_op jit(solution)/shard_map/sub | solution.py:20
  45.6 0.0 copy-start.2
  45.6 4.6 %fusion.21 = bf16[4,8,128,128]{2,3,1,0:T(8,128)(2,1)} fusion(f32[4,8,128,384]{2,3,1,0:T(8,128)} %get-tuple-element.5, f32[4,8,128]{2,1,0:T(8,128)S(1)} %get-tuple-element.4, bf16[4,2,384,128]{3,2,0,1:T(8,128)(2,1)S(1)} %constant_dynamic-update-slice_fusion), kind=kOutput, calls=%fused_computation.25 | convolution fusion | flops 406323200 | bytes 7749632 | tf_op jit(solution)/shard_map/kgtl,kld->kgtd/dot_general | solution.py:91
  50.1 0.0 collective-permute-done.3
  50.1 17.5 %all-gather.3.cloned.1.call-done = bf16[32,128,512]{1,2,0:T(8,128)(2,1)} async-done(((bf16[32,128,32]{1,2,0:T(8,128)(2,1)}), bf16[32,128,512]{1,2,0:T(8,128)(2,1)}) %all-gather.3.cloned.1.call-update) | async-done | bytes 4194320 | tf_op jit(solution)/shard_map/all_gather | solution.py:64
  67.6 0.0 copy-done.2
  67.6 10.2 %fusion.3 = f32[32,128,384]{2,1,0:T(8,128)} fusion(f32[384,32,128]{0,2,1:T(8,128)} %fusion.28, pred[128,384]{1,0:T(8,128)(4,1)S(1)} %and_and_fusion, bf16[32,128,128]{2,1,0:T(8,128)(2,1)S(1)} %copy-done, bf16[32,128,512]{1,2,0:T(8,128)(2,1)} %all-gather.3.cloned.1.call-done, bf16[128,512]{1,0:T(8,128)(2,1)S(1)} %copy-done.2, ...), kind=kOutput, calls=%fused_computation.5 | convolution fusion | flops 2155479040 | bytes 18268160 | tf_op jit(solution)/shard_map/htc,lc->htl/dot_general | solution.py:68
  77.8 6.3 %fusion.41 = f32[32,128]{1,0:T(8,128)S(1)} fusion(f32[32,128,384]{2,1,0:T(8,128)} %fusion.3), kind=kOutput, calls=%fused_computation.53 | output fusion | flops 3146111 | bytes 6307840 | tf_op jit(solution)/shard_map/sub | solution.py:20
  84.2 36.4 %all-gather.5.cloned.1.call-done = bf16[32,512,128]{2,1,0:T(8,128)(2,1)} async-done(((bf16[32,32,128]{2,1,0:T(8,128)(2,1)}), bf16[32,512,128]{2,1,0:T(8,128)(2,1)}) %all-gather.5.cloned.1.call-update) | async-done | bytes 4194320 | tf_op jit(solution)/shard_map/all_gather | solution.py:81
  120.6 14.3 %fusion.20 = (f32[128]{0:T(128)S(1)}, bf16[32,128,128]{1,2,0:T(8,128)(2,1)S(1)}) fusion(bf16[4,8,128,128]{2,3,1,0:T(8,128)(2,1)} %fusion.21, bf16[32,512,128]{2,1,0:T(8,128)(2,1)} %all-gather.5.cloned.1.call-done, f32[32,128]{1,0:T(8,128)S(1)} %fusion.41, f32[32,128,384]{2,1,0:T(8,128)} %fusion.3, bf16[128,512]{1,0:T(8,128)(2,1)S(1)} %copy-done.2, ...), kind=kOutput, calls=%fused_computation.24 | convolution fusion | flops 2158629376 | bytes 12993024 | tf_op jit(solution)/shard_map/htc,hcd->htd/dot_general | solution.py:78
  134.9 1.3 copy.16
  136.2 0.5 broadcast_multiply_fusion
  (6 shorter events, 0.1 us)
Async XLA Ops:
  7.2 33.7 %copy-start = (bf16[32,128,128]{2,1,0:T(8,128)(2,1)S(1)}, bf16[32,128,128]{2,1,0:T(8,128)(2,1)}, u32[]{:S(2)}) copy-start(bf16[32,128,128]{2,1,0:T(8,128)(2,1)} %param.8) | copy-start | bytes 3145732
  7.2 33.7 %copy-start.1 = (bf16[4,2,128,128]{3,2,1,0:T(8,128)(2,1)S(1)}, bf16[4,2,128,128]{3,2,1,0:T(8,128)(2,1)}, u32[]{:S(2)}) copy-start(bf16[4,2,128,128]{3,2,1,0:T(8,128)(2,1)} %param.10) | copy-start | bytes 786436
  7.2 60.4 %all-gather.3.cloned.1.call-start = ((), (), s32[]{:S(2)}) async-start(), calls=%async_computation | async-start | bytes 4456448 | tf_op jit(solution)/shard_map/all_gather | solution.py:64
  7.9 112.7 %all-gather.5.cloned.1.call-start = ((), (), s32[]{:S(2)}) async-start(), calls=%async_computation.1 | async-start | bytes 4456448 | tf_op jit(solution)/shard_map/all_gather | solution.py:81
  8.7 13.4 %collective-permute-start = (s32[128]{0:T(128)}, s32[128]{0:T(128)S(1)}, u32[]{:S(2)}, u32[]{:S(2)}) collective-permute-start(s32[128]{0:T(128)} %param.15), channel_id=1, source_target_pairs={{0,1},{1,2},{2,3},{3,4},{4,5},{5,6},{6,7},{7,8},{8,9},{9,10},{10,1... | collective-permute-start | bytes 1544 | tf_op jit(solution)/shard_map/ppermute | solution.py:14
  12.1 17.8 %collective-permute-start.6 = (bf16[4,2,128,128]{3,2,0,1:T(8,128)(2,1)S(1)}, bf16[4,2,128,128]{3,2,0,1:T(8,128)(2,1)S(1)}, u32[]{:S(2)}, u32[]{:S(2)}) collective-permute-start(bf16[4,2,128,128]{3,2,0,1:T(8,128)(2,1)S(1)} %copy.12), channel_id=1, source_target_pairs={{0,1},{1,2},{2,3},{3,4},{4,5},{5,6},{6,7},{7,8},{8,9},{9,10},{10,1... | collective-permute-start | bytes 786440 | tf_op jit(solution)/shard_map/ppermute | solution.py:14
  16.6 22.3 %collective-permute-start.2 = (bf16[128,512]{1,0:T(8,128)(2,1)}, bf16[128,512]{1,0:T(8,128)(2,1)S(1)}, u32[]{:S(2)}, u32[]{:S(2)}) collective-permute-start(bf16[128,512]{1,0:T(8,128)(2,1)} %param.11), channel_id=1, source_target_pairs={{0,1},{1,2},{2,3},{3,4},{4,5},{5,6},{6,7},{7,8},{8,9},{9,10},{10,1... | collective-permute-start | bytes 393224 | tf_op jit(solution)/shard_map/ppermute | solution.py:14
  18.5 7.0 %collective-permute-start.4 = (bf16[128,64]{0,1:T(8,128)(2,1)}, bf16[128,64]{0,1:T(8,128)(2,1)S(1)}, u32[]{:S(2)}, u32[]{:S(2)}) collective-permute-start(bf16[128,64]{0,1:T(8,128)(2,1)} %param.12), channel_id=1, source_target_pairs={{0,1},{1,2},{2,3},{3,4},{4,5},{5,6},{6,7},{7,8},{8,9},{9,10},{10,1... | collective-permute-start | bytes 49160 | tf_op jit(solution)/shard_map/ppermute | solution.py:14
  22.1 2.7 %collective-permute-start.1 = (s32[128]{0:T(128)S(1)}, s32[128]{0:T(128)S(1)}, u32[]{:S(2)}, u32[]{:S(2)}) collective-permute-start(s32[128]{0:T(128)S(1)} %collective-permute-done), channel_id=1, source_target_pairs={{0,1},{1,2},{2,3},{3,4},{4,5},{5,6},{6,7},{7,8},{8,9},{9,10},{10,1... | collective-permute-start | bytes 1544 | tf_op jit(solution)/shard_map/ppermute | solution.py:14
  25.5 8.6 %collective-permute-start.5 = (bf16[128,64]{0,1:T(8,128)(2,1)S(1)}, bf16[128,64]{0,1:T(8,128)(2,1)S(1)}, u32[]{:S(2)}, u32[]{:S(2)}) collective-permute-start(bf16[128,64]{0,1:T(8,128)(2,1)S(1)} %collective-permute-done.4), channel_id=1, source_target_pairs={{0,1},{1,2},{2,3},{3,4},{4,5},{5,6},{6,7},{7,8},{8,9},{9,10},{10,1... | collective-permute-start | bytes 49160 | tf_op jit(solution)/shard_map/ppermute | solution.py:14
  29.9 10.9 %collective-permute-start.7 = (bf16[4,2,128,128]{3,2,0,1:T(8,128)(2,1)S(1)}, bf16[4,2,128,128]{3,2,0,1:T(8,128)(2,1)S(1)}, u32[]{:S(2)}, u32[]{:S(2)}) collective-permute-start(bf16[4,2,128,128]{3,2,0,1:T(8,128)(2,1)S(1)} %collective-permute-done.6), channel_id=1, source_target_pairs={{0,1},{1,2},{2,3},{3,4},{4,5},{5,6},{6,7},{7,8},{8,9},{9,10},{10,1... | collective-permute-start | bytes 786440 | tf_op jit(solution)/shard_map/ppermute | solution.py:14
  38.9 11.3 %collective-permute-start.3 = (bf16[128,512]{1,0:T(8,128)(2,1)S(1)}, bf16[128,512]{1,0:T(8,128)(2,1)S(1)}, u32[]{:S(2)}, u32[]{:S(2)}) collective-permute-start(bf16[128,512]{1,0:T(8,128)(2,1)S(1)} %collective-permute-done.2), channel_id=1, source_target_pairs={{0,1},{1,2},{2,3},{3,4},{4,5},{5,6},{6,7},{7,8},{8,9},{9,10},{10,1... | collective-permute-start | bytes 393224 | tf_op jit(solution)/shard_map/ppermute | solution.py:14
  45.6 22.1 %copy-start.2 = (bf16[128,512]{1,0:T(8,128)(2,1)S(1)}, bf16[128,512]{1,0:T(8,128)(2,1)}, u32[]{:S(2)}) copy-start(bf16[128,512]{1,0:T(8,128)(2,1)} %param.11) | copy-start | bytes 393220
Sparse Core Ops, SparseCore 0:
  10.2 57.4 all-gather.2
  69.8 50.7 all-gather.4
where the time goes:
time: 144 us
  waiting for transfers between devices  56.1 us (39%)
  matrix products  38.4 us (27%)
  starting transfers between devices  23.9 us (17%)
  between operations  14.3 us (10%)
  other arithmetic  8.31 us (6%)
  local copies, waits for them, and re-layouts  2.56 us (2%)
    all_gather x1, waiting for transfers between devices, shards(): lax.all_gather(value_upward_matrix, 'ctx', axis=1, tiled=True)  36.4 us
    ppermute x8, starting transfers between devices, from_behind(): return lax.ppermute(block, axis, route)  23.8 us
    all_gather x1, waiting for transfers between devices, shards(): lax.all_gather(key_upward_matrix, 'ctx', axis=2, tiled=True)  17.5 us
    dot_general x1, matrix products, shards(): jnp.einsum('htc,hcd->htd', latent_out, lax.all_gather(value_upward_matrix...  14.3 us
    dot_general x1, matrix products, shards(): jnp.einsum('htc,lc->htl', query_latent, keys_latent, preferred_element_ty...  10.2 us
    sub x1, other arithmetic, masked_softmax(): raised = jnp.exp(scores - highest)  6.35 us
    dot_general x1, matrix products, shards(): jnp.einsum('htp,lp->htl', query_pos, keys_pos, preferred_element_type=jnp...  4.75 us
    sub x1, matrix products, masked_softmax(): raised = jnp.exp(scores - highest)  4.64 us
  transfers between devices with their start and end apart: 10, of which 3 were waited for; matrix products, arithmetic and copies ran while one was open for 23% of the time, Pallas kernels for 0%

commit v1 on v0

v1 whole, which is shorter than its diff:
```python
import functools
import math

import jax
import jax.numpy as jnp
from jax import lax
from jax.experimental import pallas as pl
from jax.experimental.pallas import tpu as pltpu
from jax.sharding import PartitionSpec as P

REACH = 2
MASKED = -1e30
CHUNK = 2
LOG2E = 1.4426950408889634


def dot(a, b, dims):
    return lax.dot_general(a, b, (dims, ((), ())), preferred_element_type=jnp.float32)


def kernel(
    n,
    q_ref, qp_ref, kv_ref, lat_ref, kp_ref, ku_ref, vu_ref, seg_ref,
    out_ref, err_ref,
    G, QB, QPB, LATB, KPB, KVB, SEGB, BIAS, TO, SO, ACC, EROW, EIN,
    lsem, psend, precv, qsend, qrecv, hsend, hrecv, ssend, srecv,
    zs, zr, ys, yr, xs, xr, osend, orecv, olsem, esend, erecv, elsem,
):
    H, T, D = q_ref.shape
    C = lat_ref.shape[1]
    PD = qp_ref.shape[1]
    KV = kv_ref.shape[0]
    w = ku_ref.shape[1]
    Hh, KVh = H // 2, KV // 2
    hc = CHUNK
    nch = Hh // hc
    per_group = (H // KV) // hc
    Z = n // 4
    i = lax.axis_index("ctx")
    d = lax.axis_index("dp")
    k = i % 2
    y = (i // 2) % 2
    z = i // 4
    x = d % 2
    sib = i + 1 - 2 * k
    ynb = i + 2 - 4 * y
    dx = d + 1 - 2 * x
    pair = i // 2
    has_prev = pair > 0
    has_next = pair < n // 2 - 1
    has_up = z < Z - 1
    has_dn = z > 0

    def at(c, dd=d):
        return {"dp": dd, "ctx": c}

    def rc(src, dst, ss, rs, dev):
        return pltpu.make_async_remote_copy(
            src_ref=src, dst_ref=dst, send_sem=ss, recv_sem=rs,
            device_id=dev, device_id_type=pl.DeviceIdType.MESH)

    bar = pltpu.get_barrier_semaphore()

    def greet(dev):
        pl.semaphore_signal(bar, inc=1, device_id=dev, device_id_type=pl.DeviceIdType.MESH)

    def one_if(c):
        return jnp.where(c, 1, 0).astype(jnp.int32)

    greet(at(sib))
    greet(at(ynb))
    greet(at(i, dx))

    @pl.when(has_up)
    def _():
        greet(at(i + 4))

    @pl.when(has_dn)
    def _():
        greet(at(i - 4))

    @pl.when(has_next)
    def _():
        greet(at(2 * pair + 2))
        greet(at(2 * pair + 3))

    @pl.when(has_prev)
    def _():
        greet(at(2 * pair - 2))
        greet(at(2 * pair - 1))

    mine = pl.ds(k * Hh, Hh)
    theirs = pl.ds((1 - k) * Hh, Hh)
    kmine = pl.ds(k * KVh, KVh)
    ktheirs = pl.ds((1 - k) * KVh, KVh)
    tl = pl.ds(pl.multiple_of((2 + k) * T, T), T)
    locals_ = [
        pltpu.make_async_copy(ku_ref.at[mine], G.at[i, 0], lsem.at[0]),
        pltpu.make_async_copy(vu_ref.at[mine], G.at[i, 1], lsem.at[1]),
        pltpu.make_async_copy(q_ref.at[mine], QB.at[k], lsem.at[2]),
        pltpu.make_async_copy(qp_ref.at[mine], QPB.at[k], lsem.at[3]),
        pltpu.make_async_copy(lat_ref, LATB.at[tl], lsem.at[4]),
        pltpu.make_async_copy(kp_ref, KPB.at[:, tl], lsem.at[5]),
        pltpu.make_async_copy(kv_ref.at[kmine], KVB.at[2 + k], lsem.at[6]),
        pltpu.make_async_copy(seg_ref, SEGB.at[2 + k], lsem.at[7]),
    ]
    for c in locals_:
        c.start()

    @pl.when(jnp.logical_not(has_prev))
    def _():
        LATB[0:2 * T] = jnp.zeros((2 * T, C), LATB.dtype)
        KPB[:, 0:2 * T] = jnp.zeros((PD, 2 * T), KPB.dtype)
        KVB[0:2] = jnp.zeros((2, KVh, 2, T, D), KVB.dtype)
        SEGB[0:2] = jnp.full((2, 1, T), -1, jnp.int32)

    pl.semaphore_wait(
        bar, 3 + one_if(has_up) + one_if(has_dn) + 2 * one_if(has_next) + 2 * one_if(has_prev))

    def p_copy(m, j):
        src = (ku_ref, vu_ref)[m]
        return rc(src.at[pl.ds((1 - k) * Hh + j * hc, hc)], G.at[i, m, pl.ds(j * hc, hc)],
                  psend.at[m, j], precv.at[m, j], at(sib))

    def p_wait(m, j):
        here = G.at[sib, m, pl.ds(j * hc, hc)]
        rc(here, here, psend.at[m, j], precv.at[m, j], at(sib)).wait_recv()

    def bundle(row, target, who, kh):
        col = pl.ds(pl.multiple_of(row * T, T), T)
        return [
            rc(lat_ref, LATB.at[col], hsend.at[who, 0], hrecv.at[row, 0], target),
            rc(kp_ref, KPB.at[:, col], hsend.at[who, 1], hrecv.at[row, 1], target),
            rc(kv_ref.at[kh], KVB.at[row], hsend.at[who, 2], hrecv.at[row, 2], target),
            rc(seg_ref, SEGB.at[row], hsend.at[who, 3], hrecv.at[row, 3], target),
        ]

    def bundle_wait(row):
        col = pl.ds(pl.multiple_of(row * T, T), T)
        for idx, ref in enumerate((LATB.at[col], KPB.at[:, col], KVB.at[row], SEGB.at[row])):
            rc(ref, ref, hsend.at[0, idx], hrecv.at[row, idx], at(sib)).wait_recv()

    q_copies = [
        rc(q_ref.at[theirs], QB.at[k], qsend.at[0], qrecv.at[0], at(sib)),
        rc(qp_ref.at[theirs], QPB.at[k], qsend.at[1], qrecv.at[1], at(sib)),
    ]
    for j in range(nch):
        for m in range(2):
            p_copy(m, j).start()
        if j == 0:
            for c in bundle(2 + k, at(sib), 0, ktheirs) + q_copies:
                c.start()

            @pl.when(has_next)
            def _():
                for t in range(2):
                    for c in bundle(k, at(2 * pair + 2 + t), 1 + t, pl.ds(t * KVh, KVh)):
                        c.start()

    for c in locals_[:2]:
        c.wait()

    def zpair(j, zz):
        return G.at[pl.ds(4 * zz + 2 * y, 2), :, pl.ds(j * hc, hc)]

    def single(j, zz, yy, xx):
        return G.at[4 * zz + 2 * yy + xx, :, pl.ds(j * hc, hc)]

    def up(j, zz):
        return rc(zpair(j, zz), zpair(j, zz), zs.at[0, j, zz], zr.at[j, zz], at(i + 4))

    def dn(j, zz):
        return rc(zpair(j, zz), zpair(j, zz), zs.at[1, j, zz], zr.at[j, zz], at(i - 4))

    def yc(j, zz):
        s = single(j, zz, y, x)
        return rc(s, s, ys.at[j, zz], yr.at[j, zz], at(ynb))

    def yc_wait(j, zz):
        s = single(j, zz, 1 - y, x)
        rc(s, s, ys.at[j, zz], yr.at[j, zz], at(ynb)).wait_recv()

    def xc(j, zz):
        s = single(j, zz, 1 - y, x)
        return rc(s, s, xs.at[j, zz], xr.at[j, zz], at(i, dx))

    def xc_wait(j, zz):
        s = single(j, zz, 1 - y, 1 - x)
        rc(s, s, xs.at[j, zz], xr.at[j, zz], at(i, dx)).wait_recv()

    def e1(j):
        for m in range(2):
            p_wait(m, j)

        @pl.when(has_up)
        def _():
            up(j, z).start()

        @pl.when(has_dn)
        def _():
            dn(j, z).start()

        yc(j, z).start()

    def e2(j, r):
        @pl.when(z - r >= 0)
        def _():
            zz = z - r
            up(j, zz).wait_recv()

            @pl.when(has_up)
            def _():
                up(j, zz).start()

            yc(j, zz).start()

        @pl.when(z + r < Z)
        def _():
            zz = z + r
            dn(j, zz).wait_recv()

            @pl.when(has_dn)
            def _():
                dn(j, zz).start()

            yc(j, zz).start()

    def e3(j, r):
        if r == 0:
            yc_wait(j, z)
            xc(j, z).start()
            return
        for sign in (-1, 1):
            zz = z + sign * r

            @pl.when((zz >= 0) & (zz < Z))
            def _():
                yc_wait(j, zz)
                xc(j, zz).start()

    def e4(j):
        for zz in range(Z):
            xc_wait(j, zz)

    def probs(s, pb, scale):
        rows = s.shape[0]
        s = (s.reshape(rows // T, T, 3 * T) + BIAS[pb][None]).reshape(rows, 3 * T)
        top = jnp.max(s, axis=-1, keepdims=True)
        e = jnp.exp2((s - top) * (scale * LOG2E))
        return e.astype(jnp.bfloat16), 1.0 / jnp.sum(e, axis=-1, keepdims=True)

    def teacher(j):
        heads = pl.ds(j * hc, hc)
        g = j // per_group
        for pb in range(2):
            q = QB[pb, heads].reshape(hc * T, D)
            keys = KVB[pb:pb + 3, g, 0].reshape(3 * T, D)
            vals = KVB[pb:pb + 3, g, 1].reshape(3 * T, D)
            e, inv = probs(dot(q, keys, ((1,), (1,))), pb, 1.0 / math.sqrt(D))
            o = dot(e, vals, ((1,), (0,))) * inv
            TO[pb, heads] = o.astype(jnp.bfloat16).reshape(hc, T, D)

    def student(j):
        qls = []
        for u in range(hc):
            h = j * hc + u
            q = QB[:, h].reshape(2 * T, D)
            up_k = G[:, 0, h].reshape(C, D)
            qls.append(dot(q, up_k, ((1,), (1,))).astype(jnp.bfloat16))
        los, invs = [], []
        for pb in range(2):
            rows = slice(pb * T, pb * T + 3 * T)
            lat = LATB[rows]
            kp = KPB[:, rows]
            ql = jnp.concatenate([a[pb * T:(pb + 1) * T] for a in qls], 0)
            pos = jnp.concatenate(
                [dot(QPB[pb, j * hc + u], kp, ((0,), (0,))) for u in range(hc)], 0)
            s = dot(ql, lat, ((1,), (1,))) + pos
            e, inv = probs(s, pb, 1.0 / math.sqrt(D + PD))
            los.append(dot(e, lat, ((1,), (0,))).astype(jnp.bfloat16))
            invs.append(inv)
        for u in range(hc):
            h = j * hc + u
            up_v = G[:, 1, h].reshape(C, D)
            cut = slice(u * T, (u + 1) * T)
            lo = jnp.concatenate([los[0][cut], los[1][cut]], 0)
            inv = jnp.concatenate([invs[0][cut], invs[1][cut]], 0)
            so = (dot(lo, up_v, ((1,), (0,))) * inv).astype(jnp.bfloat16).reshape(2, T, D)
            SO[:, h] = so
            diff = so.astype(jnp.float32) - TO[:, h].astype(jnp.float32)
            ACC[...] += diff * diff

    def o_remote(j):
        return rc(SO.at[1 - k, pl.ds(j * hc, hc)], out_ref.at[pl.ds(k * Hh + j * hc, hc)],
                  osend.at[j], orecv.at[j], at(sib))

    def o_wait(j):
        here = out_ref.at[pl.ds((1 - k) * Hh + j * hc, hc)]
        rc(here, here, osend.at[j], orecv.at[j], at(sib)).wait_recv()

    def o_local(j):
        return pltpu.make_async_copy(
            SO.at[k, pl.ds(j * hc, hc)], out_ref.at[pl.ds(k * Hh + j * hc, hc)], olsem.at[j])

    def prepare():
        for c in locals_[2:]:
            c.wait()
        for idx, ref in enumerate((QB.at[1 - k], QPB.at[1 - k])):
            rc(ref, ref, qsend.at[idx], qrecv.at[idx], at(sib)).wait_recv()
        bundle_wait(3 - k)

        @pl.when(has_prev)
        def _():
            bundle_wait(0)
            bundle_wait(1)

        ACC[...] = jnp.zeros_like(ACC)
        row = lax.broadcasted_iota(jnp.int32, (T, T), 0)
        lane = lax.broadcasted_iota(jnp.int32, (T, T), 1)
        for pb in range(2):
            own = jnp.transpose(jnp.broadcast_to(SEGB[2 + pb], (T, T)))
            for b in range(3):
                ok = jnp.broadcast_to(SEGB[pb + b], (T, T)) == own
                if b == 2:
                    ok = ok & (lane <= row)
                BIAS[pb, :, b * T:(b + 1) * T] = jnp.where(ok, 0.0, MASKED)

    last = Z + 1

    def guarded(t, lag, f):
        j = t - lag

        @pl.when((j >= 0) & (j < nch))
        def _():
            f(j)

    @pl.loop(0, nch + last + 1)
    def _(t):
        guarded(t, 0, e1)
        for r in range(1, Z):
            guarded(t, r, functools.partial(e2, r=r))
        for r in range(Z):
            guarded(t, r + 1, functools.partial(e3, r=r))
        guarded(t, last, e4)

        @pl.when(t == 1)
        def _():
            prepare()

        guarded(t, 1, teacher)

        def send_out(j):
            o_remote(j).start()
            o_local(j).start()

        guarded(t, last, student)
        guarded(t, last + 1, send_out)

    for pb in range(2):
        EROW[pb] = jnp.sum(jnp.transpose(ACC[pb]), axis=0, keepdims=True)
    e_copy = rc(EROW.at[1 - k], EIN, esend, erecv, at(sib))
    e_copy.start()

    for c in q_copies + bundle(2 + k, at(sib), 0, ktheirs):
        c.wait_send()

    @pl.when(has_next)
    def _():
        for t in range(2):
            for c in bundle(k, at(2 * pair + 2 + t), 1 + t, pl.ds(t * KVh, KVh)):
                c.wait_send()

    @pl.loop(0, nch)
    def _(j):
        for m in range(2):
            p_copy(m, j).wait_send()
        for zz in range(Z):
            @pl.when(has_up & (zz <= z))
            def _():
                up(j, zz).wait_send()

            @pl.when(has_dn & (zz >= z))
            def _():
                dn(j, zz).wait_send()

            yc(j, zz).wait_send()
            xc(j, zz).wait_send()
        o_remote(j).wait_send()
        o_local(j).wait()
        o_wait(j)

    e_copy.wait()
    EROW[k] = (EROW[k] + EIN[...]) * (1.0 / (H * D))
    done = pltpu.make_async_copy(EROW.at[k], err_ref, elsem)
    done.start()
    done.wait()


def fused(n, queries, query_pos, key_values, latent, key_pos, key_up, value_up, segment_ids):
    H, T, D = queries.shape
    C = latent.shape[1]
    PD = key_pos.shape[1]
    KV = key_values.shape[0]
    w = value_up.shape[1]
    Hh, KVh = H // 2, KV // 2
    nch = Hh // CHUNK
    Z = n // 4
    bf, f32 = jnp.bfloat16, jnp.float32
    dma = pltpu.SemaphoreType.DMA
    anywhere = pl.BlockSpec(memory_space=pl.ANY)
    out, err = pl.pallas_call(
        functools.partial(kernel, n),
        out_shape=(
            jax.ShapeDtypeStruct((H, T, D), bf),
            jax.ShapeDtypeStruct((1, T), f32),
        ),
        in_specs=[anywhere] * 8,
        out_specs=(anywhere, anywhere),
        scratch_shapes=[
            pltpu.VMEM((n, 2, Hh, w, D), bf),
            pltpu.VMEM((2, Hh, T, D), bf),
            pltpu.VMEM((2, Hh, PD, T), bf),
            pltpu.VMEM((4 * T, C), bf),
            pltpu.VMEM((PD, 4 * T), bf),
            pltpu.VMEM((4, KVh, 2, T, D), bf),
            pltpu.VMEM((4, 1, T), jnp.int32),
            pltpu.VMEM((2, T, 3 * T), f32),
            pltpu.VMEM((2, Hh, T, D), bf),
            pltpu.VMEM((2, Hh, T, D), bf),
            pltpu.VMEM((2, T, D), f32),
            pltpu.VMEM((2, 1, T), f32),
            pltpu.VMEM((1, T), f32),
            dma((8,)),
            dma((2, nch)), dma((2, nch)),
            dma((2,)), dma((2,)),
            dma((3, 4)), dma((4, 4)),
            dma((1,)), dma((1,)),
            dma((2, nch, Z)), dma((nch, Z)),
            dma((nch, Z)), dma((nch, Z)),
            dma((nch, Z)), dma((nch, Z)),
            dma((nch,)), dma((nch,)), dma((nch,)),
            dma(()), dma(()), dma(()),
        ],
        compiler_params=pltpu.CompilerParams(
            collective_id=0, has_side_effects=True, vmem_limit_bytes=56 * 1024 * 1024),
        name="latent_distill",
    )(
        queries,
        jnp.swapaxes(query_pos, 1, 2),
        key_values,
        latent,
        jnp.swapaxes(key_pos, 0, 1),
        jnp.swapaxes(key_up, 1, 2),
        value_up,
        segment_ids.reshape(1, T),
    )
    return out, err.reshape(T)


def solution(mesh):
    placed = (
        P(None, ("dp", "ctx"), None),
        P(None, ("dp", "ctx"), None),
        P(None, None, ("dp", "ctx"), None),
        P(("dp", "ctx"), None),
        P(("dp", "ctx"), None),
        P(None, None, "ctx"),
        P(None, "ctx", None),
        P(("dp", "ctx")),
    )
    return jax.shard_map(
        functools.partial(fused, mesh.shape["ctx"]),
        mesh=mesh,
        in_specs=placed,
        out_specs=(P(None, ("dp", "ctx"), None), P(("dp", "ctx"))),
        check_vma=False,
    )
```

time: 144 us -> 70.8 us (0.49)
  Pallas kernels: 0 us -> 67.2 us
  waiting for transfers between devices: 56.1 us -> 0 us
  matrix products: 38.4 us -> 0 us
  starting transfers between devices: 23.9 us -> 0 us
  between operations: 14.3 us -> 0.65 us
  other arithmetic: 8.31 us -> 0 us
    pallas_call x0 -> x1, Pallas kernels: none -> 67.2 us  [fused(): pl.pallas_call(functools.partial(kernel, n), out_shape=(jax.ShapeDtypeStr...]
    all_gather x2 -> x0, waiting for transfers between devices: 53.9 us -> none  [the longest x1 36.4 us: shards(): lax.all_gather(value_upward_matrix, 'ctx', axis=1, tiled=True)]
    dot_general x4 -> x0, matrix products: 33.8 us -> none  [the longest x1 14.3 us: shards(): jnp.einsum('htc,hcd->htd', latent_out, lax.all_gather(value_upward_matrix...]
    ppermute x8 -> x0, starting transfers between devices: 23.8 us -> none  [from_behind(): return lax.ppermute(block, axis, route)]
    sub x1 -> x0, other arithmetic: 6.35 us -> none  [masked_softmax(): raised = jnp.exp(scores - highest)]
    sub x1 -> x0, matrix products: 4.64 us -> none  [masked_softmax(): raised = jnp.exp(scores - highest)]
  transfers between devices with their start and end apart: 10 -> 0, of which waited for: 3 -> 0; matrix products, arithmetic and copies ran while one was open for 23% -> 0% of each run, Pallas kernels for 0% -> 0%
where the time goes in v1:
time: 70.8 us; the launch traced here: 70.7 us
  Pallas kernels  67.2 us (95%)
  local copies, waits for them, and re-layouts  2.82 us (4%)
    pallas_call x1, Pallas kernels, fused(): pl.pallas_call(functools.partial(kernel, n), out_shape=(jax.ShapeDtypeStr...  67.2 us
    unnamed x4, local copies, waits for them, and re-layouts  2.82 us

profile of v1, /device:TPU:0, one launch (start us, length us, event | category | flops | bytes accessed | tf_op | source)
XLA Modules:
  0.0 70.7 jit_solution(8948079277571234421)
XLA Ops:
  0.6 67.2 %latent_distill.1 = (bf16[32,128,128]{2,1,0:T(8,128)(2,1)}, f32[1,128]{1,0:T(1,128)}) custom-call(bf16[32,128,128]{2,1,0:T(8,128)(2,1)} %q_ref.1, bf16[32,64,128]{2,1,0:T(8,128)(2,1)} %bitcast.5, bf16[4,2,128,128]{3,2,1,0:T(8,128)(2,1)} %kv_ref.1, bf16[128,512]{1,0:T(8,128)(2,1)} %lat_ref.1, bf16[64,128]{1,0:T(8,128)(2,1)} %bitcast.7, ...), custom_call_target="tpu_custom_call" | custom-call | tf_op jit(solution)/shard_map/latent_distill/pallas_call | solution.py:411
  67.8 0.0 copy-start
  67.8 2.3 %copy.12 = bf16[32,128,128]{2,1,0:T(8,128)(2,1)} copy(bf16[32,128,128]{2,1,0:T(8,128)(2,1)} %get-tuple-element.8) | data formatting | bytes 2097152
  70.1 0.0 copy-done
  70.1 0.5 copy.13
Async XLA Ops:
  67.8 2.3 %copy-start = (f32[1,128]{1,0:T(1,128)S(1)}, f32[1,128]{1,0:T(1,128)}, u32[]{:S(2)}) copy-start(f32[1,128]{1,0:T(1,128)} %get-tuple-element.5) | copy-start | bytes 1540

commit v2 on v1

--- a/solution.py
+++ b/solution.py
@@ -10,7 +10,9 @@
 
 REACH = 2
 MASKED = -1e30
-CHUNK = 2
+CHUNK = 4
+AHEAD = 0
+HALO = 0
 LOG2E = 1.4426950408889634
 
 
@@ -24,7 +26,7 @@
     out_ref, err_ref,
     G, QB, QPB, LATB, KPB, KVB, SEGB, BIAS, TO, SO, ACC, EROW, EIN,
     lsem, psend, precv, qsend, qrecv, hsend, hrecv, ssend, srecv,
-    zs, zr, ys, yr, xs, xr, osend, orecv, olsem, esend, erecv, elsem,
+    zs, zr, ys, yr, xs, xr, ws, wr, osend, orecv, olsem, esend, erecv, elsem,
 ):
     H, T, D = q_ref.shape
     C = lat_ref.shape[1]
@@ -33,6 +35,7 @@
     w = ku_ref.shape[1]
     Hh, KVh = H // 2, KV // 2
     hc = CHUNK
+    early = hc // 2
     nch = Hh // hc
     per_group = (H // KV) // hc
     Z = n // 4
@@ -129,11 +132,26 @@
     def bundle(row, target, who, kh):
         col = pl.ds(pl.multiple_of(row * T, T), T)
         return [
-            rc(lat_ref, LATB.at[col], hsend.at[who, 0], hrecv.at[row, 0], target),
-            rc(kp_ref, KPB.at[:, col], hsend.at[who, 1], hrecv.at[row, 1], target),
             rc(kv_ref.at[kh], KVB.at[row], hsend.at[who, 2], hrecv.at[row, 2], target),
-            rc(seg_ref, SEGB.at[row], hsend.at[who, 3], hrecv.at[row, 3], target),
+        ] + shared(row, target, who)
+
+    def shared(row, target, who, landed=False):
+        col = pl.ds(pl.multiple_of(row * T, T), T)
+        dst = (LATB.at[col], KPB.at[:, col], SEGB.at[row])
+        src = dst if landed else (lat_ref, kp_ref, seg_ref)
+        return [
+            rc(a, b, hsend.at[who, e], hrecv.at[row, e], target)
+            for a, b, e in zip(src, dst, (0, 1, 3))
         ]
+
+    def to_next():
+        first = 2 * pair + 2
+        return shared(k, at(first + k), 1) + [
+            rc(kv_ref.at[pl.ds(t * KVh, KVh)], KVB.at[k], hsend.at[1 + t, 2],
+               hrecv.at[k, 2], at(first + t)) for t in range(2)]
+
+    def forward():
+        return shared(k, at(sib), 3, True)
 
     def bundle_wait(row):
         col = pl.ds(pl.multiple_of(row * T, T), T)
@@ -151,26 +169,48 @@
             for c in bundle(2 + k, at(sib), 0, ktheirs) + q_copies:
                 c.start()
 
-            @pl.when(has_next)
-            def _():
-                for t in range(2):
-                    for c in bundle(k, at(2 * pair + 2 + t), 1 + t, pl.ds(t * KVh, KVh)):
-                        c.start()
-
     for c in locals_[:2]:
         c.wait()
 
-    def zpair(j, zz):
-        return G.at[pl.ds(4 * zz + 2 * y, 2), :, pl.ds(j * hc, hc)]
+    def part(j, zz, xx, first, size):
+        return G.at[4 * zz + 2 * y + xx, :, pl.ds(j * hc + first, size)]
 
     def single(j, zz, yy, xx):
         return G.at[4 * zz + 2 * yy + xx, :, pl.ds(j * hc, hc)]
 
+    class Both:
+        def __init__(self, j, zz, way, dev):
+            a, b = part(j, zz, x, 0, hc), part(j, zz, 1 - x, 0, early)
+            self.copies = [
+                rc(a, a, zs.at[way, 0, j, zz], zr.at[0, j, zz], dev),
+                rc(b, b, zs.at[way, 1, j, zz], zr.at[1, j, zz], dev),
+            ]
+
+        def start(self):
+            for c in self.copies:
+                c.start()
+
+        def wait_send(self):
+            for c in self.copies:
+                c.wait_send()
+
+        def wait_recv(self):
+            for c in self.copies:
+                c.wait_recv()
+
     def up(j, zz):
-        return rc(zpair(j, zz), zpair(j, zz), zs.at[0, j, zz], zr.at[j, zz], at(i + 4))
+        return Both(j, zz, 0, at(i + 4))
 
     def dn(j, zz):
-        return rc(zpair(j, zz), zpair(j, zz), zs.at[1, j, zz], zr.at[j, zz], at(i - 4))
+        return Both(j, zz, 1, at(i - 4))
+
+    def side(j, zz):
+        s = part(j, zz, x, early, hc - early)
+        return rc(s, s, ws.at[j, zz], wr.at[j, zz], at(i, dx))
+
+    def side_wait(j, zz):
+        s = part(j, zz, 1 - x, early, hc - early)
+        rc(s, s, ws.at[j, zz], wr.at[j, zz], at(i, dx)).wait_recv()
 
     def yc(j, zz):
         s = single(j, zz, y, x)
@@ -213,6 +253,7 @@
                 up(j, zz).start()
 
             yc(j, zz).start()
+            side(j, zz).start()
 
         @pl.when(z + r < Z)
         def _():
@@ -224,6 +265,7 @@
                 dn(j, zz).start()
 
             yc(j, zz).start()
+            side(j, zz).start()
 
     def e3(j, r):
         if r == 0:
@@ -241,6 +283,10 @@
     def e4(j):
         for zz in range(Z):
             xc_wait(j, zz)
+
+            @pl.when(zz != z)
+            def _():
+                side_wait(j, zz)
 
     def probs(s, pb, scale):
         rows = s.shape[0]
@@ -311,8 +357,8 @@
 
         @pl.when(has_prev)
         def _():
-            bundle_wait(0)
-            bundle_wait(1)
+            bundle_wait(1 - k)
+            rc(KVB.at[k], KVB.at[k], hsend.at[0, 2], hrecv.at[k, 2], at(sib)).wait_recv()
 
         ACC[...] = jnp.zeros_like(ACC)
         row = lax.broadcasted_iota(jnp.int32, (T, T), 0)
@@ -325,7 +371,8 @@
                     ok = ok & (lane <= row)
                 BIAS[pb, :, b * T:(b + 1) * T] = jnp.where(ok, 0.0, MASKED)
 
-    last = Z + 1
+    ahead = AHEAD
+    last = Z + 1 + ahead
 
     def guarded(t, lag, f):
         j = t - lag
@@ -338,16 +385,28 @@
     def _(t):
         guarded(t, 0, e1)
         for r in range(1, Z):
-            guarded(t, r, functools.partial(e2, r=r))
+            guarded(t, r + ahead, functools.partial(e2, r=r))
         for r in range(Z):
-            guarded(t, r + 1, functools.partial(e3, r=r))
+            guarded(t, r + 1 + ahead, functools.partial(e3, r=r))
         guarded(t, last, e4)
 
-        @pl.when(t == 1)
+        @pl.when(has_next & (t == HALO))
+        def _():
+            for c in to_next():
+                c.start()
+
+        @pl.when(has_prev & (t == HALO + 1))
+        def _():
+            for c in shared(k, at(sib), 3, True):
+                c.wait_recv()
+            for c in forward():
+                c.start()
+
+        @pl.when(t == HALO + 2)
         def _():
             prepare()
 
-        guarded(t, 1, teacher)
+        guarded(t, HALO + 2, teacher)
 
         def send_out(j):
             o_remote(j).start()
@@ -366,9 +425,13 @@
 
     @pl.when(has_next)
     def _():
-        for t in range(2):
-            for c in bundle(k, at(2 * pair + 2 + t), 1 + t, pl.ds(t * KVh, KVh)):
-                c.wait_send()
+        for c in to_next():
+            c.wait_send()
+
+    @pl.when(has_prev)
+    def _():
+        for c in forward():
+            c.wait_send()
 
     @pl.loop(0, nch)
     def _(j):
@@ -385,6 +448,11 @@
 
             yc(j, zz).wait_send()
             xc(j, zz).wait_send()
+
+            @pl.when(zz != z)
+            def _():
+                side(j, zz).wait_send()
+
         o_remote(j).wait_send()
         o_local(j).wait()
         o_wait(j)
@@ -433,9 +501,10 @@
             dma((8,)),
             dma((2, nch)), dma((2, nch)),
             dma((2,)), dma((2,)),
-            dma((3, 4)), dma((4, 4)),
+            dma((4, 4)), dma((4, 4)),
             dma((1,)), dma((1,)),
-            dma((2, nch, Z)), dma((nch, Z)),
+            dma((2, 2, nch, Z)), dma((2, nch, Z)),
+            dma((nch, Z)), dma((nch, Z)),
             dma((nch, Z)), dma((nch, Z)),
             dma((nch, Z)), dma((nch, Z)),
             dma((nch,)), dma((nch,)), dma((nch,)),

time: 70.8 us -> 63.9 us (0.903)
  the two profiles are of different devices: /device:TPU:0 before, /device:TPU:29 now
where the time goes in v2:
time: 63.9 us; the launch traced here: 63.7 us
  Pallas kernels  60.2 us (94%)
  local copies, waits for them, and re-layouts  2.82 us (4%)
  between operations  0.65 us (1%)
    pallas_call x1, Pallas kernels, fused(): pl.pallas_call(functools.partial(kernel, n), out_shape=(jax.ShapeDtypeStr...  60.2 us
    unnamed x4, local copies, waits for them, and re-layouts  2.82 us

profile of v2, /device:TPU:29, one launch (start us, length us, event | category | flops | bytes accessed | tf_op | source)
XLA Modules:
  0.0 63.7 jit_solution(18176059043909954393)
XLA Ops:
  0.6 60.2 %latent_distill.1 = (bf16[32,128,128]{2,1,0:T(8,128)(2,1)}, f32[1,128]{1,0:T(1,128)}) custom-call(bf16[32,128,128]{2,1,0:T(8,128)(2,1)} %q_ref.1, bf16[32,64,128]{2,1,0:T(8,128)(2,1)} %bitcast.5, bf16[4,2,128,128]{3,2,1,0:T(8,128)(2,1)} %kv_ref.1, bf16[128,512]{1,0:T(8,128)(2,1)} %lat_ref.1, bf16[64,128]{1,0:T(8,128)(2,1)} %bitcast.7, ...), custom_call_target="tpu_custom_call" | custom-call | tf_op jit(solution)/shard_map/latent_distill/pallas_call | solution.py:479
  60.9 0.0 copy-start
  60.9 2.3 %copy.12 = bf16[32,128,128]{2,1,0:T(8,128)(2,1)} copy(bf16[32,128,128]{2,1,0:T(8,128)(2,1)} %get-tuple-element.8) | data formatting | bytes 2097152
  63.2 0.0 copy-done
  63.2 0.5 copy.13
Async XLA Ops:
  60.9 2.3 %copy-start = (f32[1,128]{1,0:T(1,128)S(1)}, f32[1,128]{1,0:T(1,128)}, u32[]{:S(2)}) copy-start(f32[1,128]{1,0:T(1,128)} %get-tuple-element.5) | copy-start | bytes 1540

commit v3 on v2

--- a/solution.py
+++ b/solution.py
@@ -384,10 +384,10 @@
     @pl.loop(0, nch + last + 1)
     def _(t):
         guarded(t, 0, e1)
+        for r in range(Z):
+            guarded(t, r + 1 + ahead, functools.partial(e3, r=r))
         for r in range(1, Z):
             guarded(t, r + ahead, functools.partial(e2, r=r))
-        for r in range(Z):
-            guarded(t, r + 1 + ahead, functools.partial(e3, r=r))
         guarded(t, last, e4)
 
         @pl.when(has_next & (t == HALO))

time: 63.9 us -> 61 us (0.955)
  the two profiles are of different devices: /device:TPU:29 before, /device:TPU:0 now
where the time goes in v3:
time: 61 us; the launch traced here: 60.8 us
  Pallas kernels  57.4 us (94%)
  local copies, waits for them, and re-layouts  2.82 us (5%)
  between operations  0.65 us (1%)
    pallas_call x1, Pallas kernels, fused(): pl.pallas_call(functools.partial(kernel, n), out_shape=(jax.ShapeDtypeStr...  57.4 us
    unnamed x4, local copies, waits for them, and re-layouts  2.82 us

profile of v3, /device:TPU:0, one launch (start us, length us, event | category | flops | bytes accessed | tf_op | source)
XLA Modules:
  0.0 60.8 jit_solution(9026375464305863663)
XLA Ops:
  0.6 57.4 %latent_distill.1 = (bf16[32,128,128]{2,1,0:T(8,128)(2,1)}, f32[1,128]{1,0:T(1,128)}) custom-call(bf16[32,128,128]{2,1,0:T(8,128)(2,1)} %q_ref.1, bf16[32,64,128]{2,1,0:T(8,128)(2,1)} %bitcast.5, bf16[4,2,128,128]{3,2,1,0:T(8,128)(2,1)} %kv_ref.1, bf16[128,512]{1,0:T(8,128)(2,1)} %lat_ref.1, bf16[64,128]{1,0:T(8,128)(2,1)} %bitcast.7, ...), custom_call_target="tpu_custom_call" | custom-call | tf_op jit(solution)/shard_map/latent_distill/pallas_call | solution.py:479
  58.0 0.0 copy-start
  58.0 2.3 %copy.12 = bf16[32,128,128]{2,1,0:T(8,128)(2,1)} copy(bf16[32,128,128]{2,1,0:T(8,128)(2,1)} %get-tuple-element.8) | data formatting | bytes 2097152
  60.3 0.0 copy-done
  60.3 0.5 copy.13
Async XLA Ops:
  58.0 2.3 %copy-start = (f32[1,128]{1,0:T(1,128)S(1)}, f32[1,128]{1,0:T(1,128)}, u32[]{:S(2)}) copy-start(f32[1,128]{1,0:T(1,128)} %get-tuple-element.5) | copy-start | bytes 1540

commit v4 on v3

--- a/solution.py
+++ b/solution.py
@@ -386,7 +386,7 @@
         guarded(t, 0, e1)
         for r in range(Z):
             guarded(t, r + 1 + ahead, functools.partial(e3, r=r))
-        for r in range(1, Z):
+        for r in range(Z - 1, 0, -1):
             guarded(t, r + ahead, functools.partial(e2, r=r))
         guarded(t, last, e4)
 

time: 61 us -> 62.3 us (1.021)
  Pallas kernels: 57.4 us -> 58.7 us
    pallas_call x1, Pallas kernels: 57.4 us -> 58.7 us  [fused(): pl.pallas_call(functools.partial(kernel, n), out_shape=(jax.ShapeDtypeStr...]
where the time goes in v4:
time: 62.3 us; the launch traced here: 62.2 us
  Pallas kernels  58.7 us (94%)
  local copies, waits for them, and re-layouts  2.82 us (5%)
  between operations  0.65 us (1%)
    pallas_call x1, Pallas kernels, fused(): pl.pallas_call(functools.partial(kernel, n), out_shape=(jax.ShapeDtypeStr...  58.7 us
    unnamed x4, local copies, waits for them, and re-layouts  2.82 us

profile of v4, /device:TPU:0, one launch (start us, length us, event | category | flops | bytes accessed | tf_op | source)
XLA Modules:
  0.0 62.2 jit_solution(13526873947683189486)
XLA Ops:
  0.6 58.7 %latent_distill.1 = (bf16[32,128,128]{2,1,0:T(8,128)(2,1)}, f32[1,128]{1,0:T(1,128)}) custom-call(bf16[32,128,128]{2,1,0:T(8,128)(2,1)} %q_ref.1, bf16[32,64,128]{2,1,0:T(8,128)(2,1)} %bitcast.5, bf16[4,2,128,128]{3,2,1,0:T(8,128)(2,1)} %kv_ref.1, bf16[128,512]{1,0:T(8,128)(2,1)} %lat_ref.1, bf16[64,128]{1,0:T(8,128)(2,1)} %bitcast.7, ...), custom_call_target="tpu_custom_call" | custom-call | tf_op jit(solution)/shard_map/latent_distill/pallas_call | solution.py:479
  59.3 0.0 copy-start
  59.3 2.3 %copy.12 = bf16[32,128,128]{2,1,0:T(8,128)(2,1)} copy(bf16[32,128,128]{2,1,0:T(8,128)(2,1)} %get-tuple-element.8) | data formatting | bytes 2097152
  61.6 0.0 copy-done
  61.6 0.5 copy.13
Async XLA Ops:
  59.3 2.3 %copy-start = (f32[1,128]{1,0:T(1,128)S(1)}, f32[1,128]{1,0:T(1,128)}, u32[]{:S(2)}) copy-start(f32[1,128]{1,0:T(1,128)} %get-tuple-element.5) | copy-start | bytes 1540
